TPU v7x, 512 devices: a whole 4x8x8 slice. The times are simulated.
512 devices in a mesh: layer: 32 (over z_lo, x, core), dp: 8 (over y), mp: 2 (over z_hi).
Axes of the slice: x: 4, y: 8, z: 8 (z_hi: 2, z_lo: 4; z = z_hi * 4 + z_lo), core: 2. Of those that a mesh axis runs over, the one named last changes fastest.
Arguments:
- states: bfloat16 [128, 1024, 1024], P('layer', 'dp'), may hold values from -6 to 6
- weights: bfloat16 [128, 1024, 1024], P('layer', 'dp', 'mp'), may hold values from -0.1875 to 0.1875
- guess_points: bfloat16 [32, 1024, 1024], P('layer', 'dp'), may hold values from -2 to 2
- cotangent: bfloat16 [1024, 1024], P('dp'), may hold values from -6 to 6
Outputs:
- adjoint: bfloat16 [128, 1024, 1024], P('layer', 'dp', 'mp')
- weight_grads: float32 [128, 1024, 1024], P('layer', 'dp', 'mp')
All inputs are finite; a program needn't handle non-finite values.
Results may differ from a plain program's by a relative error of at most 0.03.
Values may be sent and summed in bfloat16 or wider, within the bound.
No kernel may reach another device: no remote copies, remote signals or barrier semaphores. Data moves between devices by JAX's collectives and lax.ppermute only.
A program may use at most 64 MiB of HBM per device.

v0:
```python
import jax
import jax.numpy as jnp
from jax import lax
from jax.sharding import PartitionSpec as P

step_size = 0.1


def from_behind(value, axis, steps):
    count = lax.axis_size(axis)
    leading, last = (max(0, -steps), min(count, count - steps))
    return lax.ppermute(value, axis, [(source, source + steps) for source in range(leading, last)])


def shortened(array):
    return jax.tree.map(lambda a: a.astype(jnp.bfloat16) if a.dtype == jnp.float32 else a, array)


def slope_of(inputs, weight_block):
    tangent = jnp.tanh(jnp.dot(inputs, weight_block, preferred_element_type=jnp.float32))
    return 1.0 - tangent * tangent


def back_product(scaled_rows, weight_block):
    return lax.dot_general(
        scaled_rows, weight_block, (((1,), (1,)), ((), ())), preferred_element_type=jnp.float32
    )


def body(states, weights, guess_points, cotangent):
    slab_count = lax.axis_size("layer")
    slab_index = lax.axis_index("layer")
    half_index = lax.axis_index("mp")
    layer_count, row_count, model_width = states.shape
    point_count = guess_points.shape[0]
    factor = layer_count // point_count
    columns = weights.shape[2]
    half_rows = row_count // lax.axis_size("mp")
    row_start = half_index * half_rows
    col_start = half_index * columns
    gathered = lax.all_gather(weights, "dp", axis=1, tiled=True)
    next_point = from_behind(guess_points[0], "layer", -1)
    terminal = jnp.where(
        slab_index == slab_count - 1, cotangent.astype(jnp.float32), next_point.astype(jnp.float32)
    )
    guess_wide = guess_points.astype(jnp.float32)
    slopes = [slope_of(states[layer_id], gathered[layer_id]) for layer_id in range(layer_count)]

    def scale_columns(upper_adj, layer_id):
        own_part = lax.dynamic_slice_in_dim(upper_adj, col_start, columns, 1)
        return (own_part * slopes[layer_id]).astype(jnp.bfloat16)

    def fine_step(upper_adj, scaled_rows, layer_id):
        summed = lax.psum(back_product(scaled_rows, gathered[layer_id]), "mp")
        return upper_adj + step_size * summed

    upper_adj = terminal
    residuals = [None] * point_count
    for layer_id in range(layer_count - 1, -1, -1):
        relaxed = fine_step(upper_adj, scale_columns(upper_adj, layer_id), layer_id)
        if layer_id % factor == 0:
            residuals[layer_id // factor] = relaxed - guess_wide[layer_id // factor]
            upper_adj = guess_wide[layer_id // factor]
        else:
            upper_adj = relaxed
    residual_half = lax.dynamic_slice_in_dim(jnp.stack(residuals), row_start, half_rows, 1)
    coarse_weights = lax.all_gather(gathered[::factor], "mp", axis=2, tiled=True)
    state_half = lax.dynamic_slice_in_dim(states[::factor], row_start, half_rows, 1)
    coarse_slopes = jnp.stack([slope_of(state_half[0], coarse_weights[0])])

    def coarse_solve(incoming):
        carried = incoming.astype(jnp.float32)
        results = [None] * point_count
        scaled_rows = (carried * coarse_slopes[0]).astype(jnp.bfloat16)
        stepped = (
            carried
            + factor * step_size * back_product(scaled_rows, coarse_weights[0])
            + residual_half[0]
        )
        results[0] = stepped.astype(jnp.bfloat16)
        return jnp.stack(results)

    def solve_pair(operand_pair):
        return coarse_solve(operand_pair[0])

    def keep_pair(operand_pair):
        return operand_pair[1]

    def one_turn(turn_id, loop_state):
        incoming, errors = loop_state
        errors = lax.cond(
            turn_id == slab_count - 1 - slab_index, solve_pair, keep_pair, (incoming, errors)
        )
        incoming = from_behind(shortened(errors[0]), "layer", -1)
        return (incoming, errors)

    start_in = jnp.zeros((half_rows, model_width), jnp.bfloat16)
    start_errors = jnp.zeros((point_count, half_rows, model_width), jnp.bfloat16)
    incoming, errors = lax.fori_loop(0, slab_count - 1, one_turn, (start_in, start_errors))
    errors = lax.cond(slab_index == 0, solve_pair, keep_pair, (incoming, errors))
    adjoint_parts = [None] * layer_count
    scaled_parts = [None] * layer_count
    spread = lax.all_gather(
        shortened(jnp.concatenate([errors, incoming[None]], 0)), "mp", axis=1, tiled=True
    )
    upper_adj = terminal + spread[point_count].astype(jnp.float32)
    for layer_id in range(layer_count - 1, -1, -1):
        scaled_rows = scale_columns(upper_adj, layer_id)
        if layer_id % factor == 0:
            current = guess_wide[layer_id // factor] + spread[layer_id // factor].astype(
                jnp.float32
            )
        else:
            current = fine_step(upper_adj, scaled_rows, layer_id)
        adjoint_parts[layer_id] = lax.dynamic_slice_in_dim(current, col_start, columns, 1).astype(
            jnp.bfloat16
        )
        scaled_parts[layer_id] = scaled_rows
        upper_adj = current
    adjoint_out = jnp.stack(adjoint_parts)
    scaled_out = jnp.stack(scaled_parts)
    partial_terms = jnp.einsum(
        "lrd,lrh->ldh", states, scaled_out, preferred_element_type=jnp.float32
    )
    weight_grads = step_size * lax.psum_scatter(
        partial_terms.astype(jnp.bfloat16), "dp", scatter_dimension=1, tiled=True
    ).astype(jnp.float32)
    return (adjoint_out, weight_grads)


def solution(mesh):
    return jax.shard_map(
        body,
        mesh=mesh,
        in_specs=(
            P("layer", "dp", None),
            P("layer", "dp", "mp"),
            P("layer", "dp", None),
            P("dp", None),
        ),
        out_specs=(P("layer", "dp", "mp"), P("layer", "dp", "mp")),
        check_vma=False,
    )
```

profile of v0, /device:TPU:1, one launch (start us, length us, event | category | flops | bytes accessed | tf_op | source)
XLA Modules:
  0.0 934.7 jit_solution(8836864910243469288)
XLA Ops:
  8.0 8.7 collective-permute-start.1
  19.1 53.4 %all-gather.3.cloned.1.call-done = bf16[4,1024,512]{2,1,0:T(8,128)(2,1)} async-done(((bf16[4,128,512]{2,1,0:T(8,128)(2,1)}), bf16[4,1024,512]{2,1,0:T(8,128)(2,1)}) %all-gather.3.cloned.1.call-update) | async-done | bytes 4194320 | tf_op jit(solution)/shard_map/all_gather | solution.py:41
  78.4 59.1 %all-reduce.8.cloned.1.call-done = f32[128,1024]{1,0:T(8,128)} async-done(((f32[128,1024]{1,0:T(8,128)}), f32[128,1024]{1,0:T(8,128)}) %all-reduce.8.cloned.1.call-update) | async-done | bytes 524304 | tf_op jit(solution)/shard_map/psum | solution.py:54
  142.7 56.4 %all-reduce.10.cloned.1.call-done = f32[128,1024]{1,0:T(8,128)} async-done(((f32[128,1024]{1,0:T(8,128)}), f32[128,1024]{1,0:T(8,128)}) %all-reduce.10.cloned.1.call-update) | async-done | bytes 524304 | tf_op jit(solution)/shard_map/psum | solution.py:54
  207.4 53.4 %all-reduce.12.cloned.1.call-done = f32[128,1024]{1,0:T(8,128)} async-done(((f32[128,1024]{1,0:T(8,128)}), f32[128,1024]{1,0:T(8,128)}) %all-reduce.12.cloned.1.call-update) | async-done | bytes 524304 | tf_op jit(solution)/shard_map/psum | solution.py:54
  265.6 62.4 %all-gather.5.cloned.1.call-done = bf16[1,1024,1024]{2,1,0:T(8,128)(2,1)} async-done(((bf16[1,1024,512]{2,1,0:T(8,128)(2,1)}), bf16[1,1024,1024]{2,1,0:T(8,128)(2,1)}) %all-gather.5.cloned.1.call-update) | async-done | bytes 2097168 | tf_op jit(solution)/shard_map/all_gather | solution.py:67
  330.0 59.3 %all-reduce.14.cloned.1.call-done = f32[128,1024]{1,0:T(8,128)} async-done(((f32[128,1024]{1,0:T(8,128)}), f32[128,1024]{1,0:T(8,128)}) %all-reduce.14.cloned.1.call-update) | async-done | bytes 524304 | tf_op jit(solution)/shard_map/psum | solution.py:54
  390.3 250.6 %while.23 = (s32[]{:T(128)}, bf16[64,1024]{1,0:T(8,128)(2,1)S(1)}, bf16[1,64,1024]{2,1,0:T(8,128)(2,1)S(1)}, s32[]{:T(128)}, f32[64,1024]{1,0:T(8,128)S(1)}, /*i...) while((s32[]{:T(128)}, bf16[64,1024]{1,0:T(8,128)(2,1)S(1)}, ...), condition=%wide.region_7.8_spmd, body=%wide.region_4.7_spmd.sunk | while | flops 134742016 | bytes 3408051 | solution.py:99
  390.4 2.7 collective-permute-start
  393.1 3.9 collective-permute-done
  398.9 4.4 collective-permute-done
  405.2 4.4 collective-permute-done
  411.5 4.4 collective-permute-done
  417.7 4.4 collective-permute-done
  424.0 4.4 collective-permute-done
  430.3 4.4 collective-permute-done
  436.6 4.4 collective-permute-done
  442.8 4.4 collective-permute-done
  449.1 4.4 collective-permute-done
  455.4 4.4 collective-permute-done
  461.7 5.5 collective-permute-done
  469.0 6.5 collective-permute-done
  477.4 6.5 collective-permute-done
  485.8 6.5 collective-permute-done
  494.2 6.5 collective-permute-done
  502.6 6.5 collective-permute-done
  511.0 6.5 collective-permute-done
  519.4 6.5 collective-permute-done
  527.7 6.5 collective-permute-done
  536.1 6.5 collective-permute-done
  544.5 6.5 collective-permute-done
  552.9 6.5 collective-permute-done
  561.3 6.5 collective-permute-done
  569.7 6.5 collective-permute-done
  578.1 6.5 collective-permute-done
  586.5 6.5 collective-permute-done
  594.8 6.5 collective-permute-done
  603.2 6.5 collective-permute-done
  611.6 20.7 %collective-permute-done = bf16[64,1024]{1,0:T(8,128)(2,1)S(1)} collective-permute-done((bf16[64,1024]{1,0:T(8,128)(2,1)S(1)}, bf16[64,1024]{1,0:T(8,128)(2,1)S(1)}, u32[]{:S(2)}, u32[]{:S(2)}) %collective-permute-start) | collective-permute-done | bytes 131104 | tf_op jit(solution)/shard_map/while/body/eval_jaxpr/ppermute | solution.py:12
  636.6 4.4 collective-permute-done
  641.0 15.2 %all_gather.11 = bf16[2,128,1024]{2,1,0:T(8,128)(2,1)S(1)} all-gather(bf16[2,64,1024]{2,1,0:T(8,128)(2,1)S(1)} %pad_maximum_fusion.1), channel_id=1, replica_groups=mesh['layer'=32,'dp'=8,'mp'=2] {'mp'}, dimensions={1}, use_global_device_ids=true | all-gather | bytes 786432 | tf_op jit(solution)/shard_map/all_gather | solution.py:103
  658.9 69.1 %all-reduce.16.cloned.1.call-done = f32[128,1024]{1,0:T(8,128)} async-done(((f32[128,1024]{1,0:T(8,128)}), f32[128,1024]{1,0:T(8,128)}) %all-reduce.16.cloned.1.call-update) | async-done | bytes 524304 | tf_op jit(solution)/shard_map/psum | solution.py:54
  731.7 58.0 %all-reduce.18.cloned.1.call-done = f32[128,1024]{1,0:T(8,128)} async-done(((f32[128,1024]{1,0:T(8,128)}), f32[128,1024]{1,0:T(8,128)}) %all-reduce.18.cloned.1.call-update) | async-done | bytes 524304 | tf_op jit(solution)/shard_map/psum | solution.py:54
  793.4 58.0 %all-reduce.20.cloned.1.call-done = f32[128,1024]{1,0:T(8,128)} async-done(((f32[128,1024]{1,0:T(8,128)}), f32[128,1024]{1,0:T(8,128)}) %all-reduce.20.cloned.1.call-update) | async-done | bytes 524304 | tf_op jit(solution)/shard_map/psum | solution.py:54
  852.4 4.5 convert_bitcast_fusion
  856.9 7.8 copy.11
  864.7 5.6 copy.13
  871.3 53.3 %reduce-scatter.4.cloned.1.call-done = bf16[128,2048]{1,0:T(8,128)(2,1)} async-done(((bf16[1024,2048]{1,0:T(8,128)(2,1)}), bf16[128,2048]{1,0:T(8,128)(2,1)}) %reduce-scatter.4.cloned.1.call-update) | async-done | bytes 524304
  (132 shorter events, 107.6 us)
Async XLA Ops:
  7.2 69.6 %copy-start = (bf16[4,128,1024]{2,1,0:T(8,128)(2,1)S(1)}, bf16[4,128,1024]{2,1,0:T(8,128)(2,1)}, u32[]{:S(2)}) copy-start(bf16[4,128,1024]{2,1,0:T(8,128)(2,1)} %param.10) | copy-start | bytes 3145732
  7.2 65.3 %all-gather.3.cloned.1.call-start = ((), (), s32[]{:S(2)}) async-start(), calls=%async_computation.1 | async-start | bytes 4718592 | tf_op jit(solution)/shard_map/all_gather | solution.py:41
  7.9 129.6 %all-reduce.8.cloned.1.call-start = ((), (), s32[]{:S(2)}) async-start(), calls=%async_computation.3 | async-start | bytes 1048576 | tf_op jit(solution)/shard_map/psum | solution.py:54
  8.0 10.1 %collective-permute-start.1 = (bf16[128,1024]{1,0:T(8,128)(2,1)}, bf16[128,1024]{1,0:T(8,128)(2,1)S(1)}, u32[]{:S(2)}, u32[]{:S(2)}) collective-permute-start(bf16[128,1024]{1,0:T(8,128)(2,1)} %bitcast.126), channel_id=1, source_target_pairs={{16,0},{32,16},{48,32},{64,48},{80,64},{96,80},{112,96},{128,112},... | collective-permute-start | bytes 786440 | tf_op jit(solution)/shard_map/ppermute | solution.py:12
  74.1 4.2 copy-start.1
  76.8 122.4 %all-reduce.10.cloned.1.call-start = ((), (), s32[]{:S(2)}) async-start(), calls=%async_computation.4 | async-start | bytes 1048576 | tf_op jit(solution)/shard_map/psum | solution.py:54
  141.1 119.7 %all-reduce.12.cloned.1.call-start = ((), (), s32[]{:S(2)}) async-start(), calls=%async_computation.5 | async-start | bytes 1048576 | tf_op jit(solution)/shard_map/psum | solution.py:54
  202.8 125.2 %all-gather.5.cloned.1.call-start = ((), (), s32[]{:S(2)}) async-start(), calls=%async_computation.2 | async-start | bytes 3145728 | tf_op jit(solution)/shard_map/all_gather | solution.py:67
  205.1 122.9 %slice-start = ((bf16[4,128,1024]{2,1,0:T(8,128)(2,1)}), bf16[1,128,1024]{2,1,0:T(8,128)(2,1)S(1)}, s32[]{:S(2)}) async-start(bf16[4,128,1024]{2,1,0:T(8,128)(2,1)} %param.10), calls=%async_computation.11 | async-start | bytes 524288 | tf_op jit(solution)/shard_map/slice | solution.py:68
  205.1 184.2 %all-reduce.14.cloned.1.call-start = ((), (), s32[]{:S(2)}) async-start(), calls=%async_computation.6 | async-start | bytes 1048576 | tf_op jit(solution)/shard_map/psum | solution.py:54
  264.5 463.5 %all-reduce.16.cloned.1.call-start = ((), (), s32[]{:S(2)}) async-start(), calls=%async_computation.7 | async-start | bytes 1048576 | tf_op jit(solution)/shard_map/psum | solution.py:54
  390.4 6.6 collective-permute-start
  397.0 6.3 collective-permute-start
  403.3 6.3 collective-permute-start
  409.5 6.3 collective-permute-start
  415.8 6.3 collective-permute-start
  422.1 6.3 collective-permute-start
  428.4 6.3 collective-permute-start
  434.6 6.3 collective-permute-start
  440.9 6.3 collective-permute-start
  447.2 6.3 collective-permute-start
  453.5 6.3 collective-permute-start
  459.8 7.4 collective-permute-start
  467.1 8.4 collective-permute-start
  475.5 8.4 collective-permute-start
  483.9 8.4 collective-permute-start
  492.3 8.4 collective-permute-start
  500.7 8.4 collective-permute-start
  509.1 8.4 collective-permute-start
  517.4 8.4 collective-permute-start
  525.8 8.4 collective-permute-start
  534.2 8.4 collective-permute-start
  542.6 8.4 collective-permute-start
  551.0 8.4 collective-permute-start
  559.4 8.4 collective-permute-start
  567.8 8.4 collective-permute-start
  576.1 8.4 collective-permute-start
  584.5 8.4 collective-permute-start
  592.9 8.4 collective-permute-start
  601.3 8.4 collective-permute-start
  609.7 22.6 %collective-permute-start = (bf16[64,1024]{1,0:T(8,128)(2,1)S(1)}, bf16[64,1024]{1,0:T(8,128)(2,1)S(1)}, u32[]{:S(2)}, u32[]{:S(2)}) collective-permute-start(bf16[64,1024]{1,0:T(8,128)(2,1)S(1)} %bitcast.125), channel_id=1, source_target_pairs={{16,0},{32,16},{48,32},{64,48},{80,64},{96,80},{112,96},{128,112},... | collective-permute-start | bytes 393224 | tf_op jit(solution)/shard_map/while/body/eval_jaxpr/ppermute | solution.py:12
  634.6 6.3 collective-permute-start
  640.9 15.3 %copy-start.2 = (f32[128,512]{1,0:T(8,128)S(1)}, f32[128,512]{1,0:T(8,128)}, u32[]{:S(2)}) copy-start(f32[128,512]{1,0:T(8,128)} %copy-done.1) | copy-start | bytes 786436
  658.8 192.6 %copy-start.3 = (f32[128,512]{1,0:T(8,128)S(1)}, f32[128,512]{1,0:T(8,128)}, u32[]{:S(2)}) copy-start(f32[128,512]{1,0:T(8,128)} %fusion.56) | copy-start | bytes 786436
  658.9 130.8 %all-reduce.18.cloned.1.call-start = ((), (), s32[]{:S(2)}) async-start(), calls=%async_computation.8 | async-start | bytes 1048576 | tf_op jit(solution)/shard_map/psum | solution.py:54
  731.7 119.7 %all-reduce.20.cloned.1.call-start = ((), (), s32[]{:S(2)}) async-start(), calls=%async_computation.9 | async-start | bytes 1048576 | tf_op jit(solution)/shard_map/psum | solution.py:54
  793.4 131.2 %reduce-scatter.4.cloned.1.call-start = ((), (), s32[]{:S(2)}) async-start(), calls=%async_computation.10 | async-start | bytes 4718592
Sparse Core Ops, SparseCore 0:
  10.1 62.3 all-gather.2
  76.9 60.5 all-reduce.7
  141.2 57.8 all-reduce.9
  202.9 57.8 all-reduce.11
  263.3 64.5 all-gather.4
  331.3 57.9 all-reduce.13
  659.0 68.9 all-reduce.15
  731.8 57.8 all-reduce.17
  793.5 57.8 all-reduce.19
  870.4 54.0 reduce-scatter.3
where the time goes:
time: 937 us; the launch traced here: 935 us
  waiting for transfers between devices  772 us (82%)
  starting transfers between devices  69.2 us (7%)
  matrix products  33.6 us (4%)
  local copies, waits for them, and re-layouts  18.9 us (2%)
  blocking collectives  15.2 us (2%)
  between operations  14.4 us (2%)
  other arithmetic  10.7 us (1%)
    psum x7, waiting for transfers between devices, fine_step(): summed = lax.psum(back_product(scaled_rows, gathered[layer_id]), 'mp')  413 us
    ppermute x32, waiting for transfers between devices, from_behind(): lax.ppermute(value, axis, [(source, source + steps) for source in range(l...  189 us
    ppermute x32, starting transfers between devices, from_behind(): lax.ppermute(value, axis, [(source, source + steps) for source in range(l...  68.8 us
    all_gather x1, waiting for transfers between devices, body(): lax.all_gather(gathered[::factor], 'mp', axis=2, tiled=True)  62.4 us
    unnamed x11, waiting for transfers between devices  54.1 us
    all_gather x1, waiting for transfers between devices, body(): gathered = lax.all_gather(weights, 'dp', axis=1, tiled=True)  53.4 us
    dot_general x8, matrix products, back_product(): lax.dot_general(scaled_rows, weight_block, (((1,), (1,)), ((), ())), pref...  20 us
  transfers between devices with their start and end apart: 42, of which 42 were waited for; matrix products, arithmetic and copies ran while one was open for 2% of the time, Pallas kernels for 0%

commit v1 on v0

--- a/solution.py
+++ b/solution.py
@@ -38,7 +38,15 @@
     half_rows = row_count // lax.axis_size("mp")
     row_start = half_index * half_rows
     col_start = half_index * columns
-    gathered = lax.all_gather(weights, "dp", axis=1, tiled=True)
+
+    def play_goods(buf, lane_axis, dim_k):
+        w_next = jax.lax.axis_size(lane_axis)
+        long_array = jnp.stack(w_next * [buf], axis=0)
+        p_next = jax.lax.all_to_all(long_array, lane_axis, 0, 0)
+        far_arr = jnp.concatenate(p_next, axis=dim_k)
+        return far_arr
+
+    gathered = play_goods(weights, "dp", 1)
     next_point = from_behind(guess_points[0], "layer", -1)
     terminal = jnp.where(
         slab_index == slab_count - 1, cotangent.astype(jnp.float32), next_point.astype(jnp.float32)

time: 937 us -> 989 us (1.055)
  waiting for transfers between devices: 772 us -> 816 us
  matrix products: 33.6 us -> 22.5 us
  local copies, waits for them, and re-layouts: 18.9 us -> 29.7 us
    all_to_all x0 -> x1, waiting for transfers between devices: none -> 83.8 us  [play_goods(): p_next = jax.lax.all_to_all(long_array, lane_axis, 0, 0)]
    all_gather x1 -> x0, waiting for transfers between devices: 53.4 us -> none  [body(): gathered = lax.all_gather(weights, 'dp', axis=1, tiled=True)]
    unnamed x14 -> x64, local copies, waits for them, and re-layouts: 16.6 us -> 21.8 us
    unnamed x11 -> x10, waiting for transfers between devices: 54.1 us -> 52.8 us
  transfers between devices with their start and end apart: 42 -> 42, of which waited for: 42 -> 42; matrix products, arithmetic and copies ran while one was open for 2% -> 1% of each run, Pallas kernels for 0% -> 0%
where the time goes in v1:
time: 989 us; the launch traced here: 987 us
  waiting for transfers between devices  816 us (83%)
  starting transfers between devices  73.8 us (7%)
  local copies, waits for them, and re-layouts  29.7 us (3%)
  matrix products  22.5 us (2%)
  blocking collectives  15.3 us (2%)
  other arithmetic  14.4 us (1%)
  between operations  14.2 us (1%)
    psum x7, waiting for transfers between devices, fine_step(): summed = lax.psum(back_product(scaled_rows, gathered[layer_id]), 'mp')  420 us
    ppermute x32, waiting for transfers between devices, from_behind(): lax.ppermute(value, axis, [(source, source + steps) for source in range(l...  197 us
    all_to_all x1, waiting for transfers between devices, play_goods(): p_next = jax.lax.all_to_all(long_array, lane_axis, 0, 0)  83.8 us
    ppermute x32, starting transfers between devices, from_behind(): lax.ppermute(value, axis, [(source, source + steps) for source in range(l...  65.7 us
    all_gather x1, waiting for transfers between devices, body(): lax.all_gather(gathered[::factor], 'mp', axis=2, tiled=True)  62.5 us
    unnamed x10, waiting for transfers between devices  52.8 us
    unnamed x64, local copies, waits for them, and re-layouts  21.8 us
  transfers between devices with their start and end apart: 42, of which 42 were waited for; matrix products, arithmetic and copies ran while one was open for 1% of the time, Pallas kernels for 0%

profile of v1, /device:TPU:1, one launch (start us, length us, event | category | flops | bytes accessed | tf_op | source)
XLA Modules:
  0.0 986.8 jit_solution(5481136650381966621)
XLA Ops:
  10.7 7.8 all-to-all-start
  18.5 5.7 collective-permute-start.1
  27.8 83.8 %all-to-all-done = bf16[8,4,128,512]{3,2,1,0:T(8,128)(2,1)} async-done(((bf16[8,4,128,512]{3,2,1,0:T(8,128)(2,1)}), bf16[8,4,128,512]{3,2,1,0:T(8,128)(2,1)}, u32[]{:S(2)}, u32[]{:S(2)}) %all-to-all-start) | async-done | bytes 4194336 | tf_op jit(solution)/shard_map/all_to_all | solution.py:45
  119.3 63.1 %all-reduce.8.cloned.1.call-done = f32[128,1024]{1,0:T(8,128)} async-done(((f32[128,1024]{1,0:T(8,128)}), f32[128,1024]{1,0:T(8,128)}) %all-reduce.8.cloned.1.call-update) | async-done | bytes 524304 | tf_op jit(solution)/shard_map/psum | solution.py:62
  186.2 57.6 %all-reduce.10.cloned.1.call-done = f32[128,1024]{1,0:T(8,128)} async-done(((f32[128,1024]{1,0:T(8,128)}), f32[128,1024]{1,0:T(8,128)}) %all-reduce.10.cloned.1.call-update) | async-done | bytes 524304 | tf_op jit(solution)/shard_map/psum | solution.py:62
  248.6 56.4 %all-reduce.12.cloned.1.call-done = f32[128,1024]{1,0:T(8,128)} async-done(((f32[128,1024]{1,0:T(8,128)}), f32[128,1024]{1,0:T(8,128)}) %all-reduce.12.cloned.1.call-update) | async-done | bytes 524304 | tf_op jit(solution)/shard_map/psum | solution.py:62
  309.8 62.5 %all-gather.2.cloned.1.call-done = bf16[1,1024,1024]{2,1,0:T(8,128)(2,1)} async-done(((bf16[1,1024,512]{2,1,0:T(8,128)(2,1)}), bf16[1,1024,1024]{2,1,0:T(8,128)(2,1)}) %all-gather.2.cloned.1.call-update) | async-done | bytes 2097168 | tf_op jit(solution)/shard_map/all_gather | solution.py:75
  375.2 57.8 %all-reduce.14.cloned.1.call-done = f32[128,1024]{1,0:T(8,128)} async-done(((f32[128,1024]{1,0:T(8,128)}), f32[128,1024]{1,0:T(8,128)}) %all-reduce.14.cloned.1.call-update) | async-done | bytes 524304 | tf_op jit(solution)/shard_map/psum | solution.py:62
  434.8 257.1 %while.23 = (s32[]{:T(128)}, bf16[64,1024]{1,0:T(8,128)(2,1)S(1)}, bf16[1,64,1024]{2,1,0:T(8,128)(2,1)}, s32[]{:T(128)}, f32[64,1024]{1,0:T(8,128)}, /*index=5*/...) while((s32[]{:T(128)}, bf16[64,1024]{1,0:T(8,128)(2,1)S(1)}, ...), condition=%wide.region_7.8_spmd, body=%wide.region_4.7_spmd.sunk | while | flops 134742016 | bytes 3408051 | solution.py:107
  437.6 4.1 collective-permute-done
  443.6 4.6 collective-permute-done
  450.1 4.6 collective-permute-done
  456.6 4.6 collective-permute-done
  463.0 4.6 collective-permute-done
  469.5 4.6 collective-permute-done
  476.0 4.6 collective-permute-done
  482.5 4.6 collective-permute-done
  489.0 4.6 collective-permute-done
  495.5 4.6 collective-permute-done
  502.0 4.6 collective-permute-done
  508.4 5.7 collective-permute-done
  516.0 6.7 collective-permute-done
  524.6 6.7 collective-permute-done
  533.2 6.7 collective-permute-done
  541.8 6.7 collective-permute-done
  550.4 6.7 collective-permute-done
  559.0 6.7 collective-permute-done
  567.6 6.7 collective-permute-done
  576.2 6.7 collective-permute-done
  584.8 6.7 collective-permute-done
  593.4 6.7 collective-permute-done
  602.0 6.7 collective-permute-done
  610.6 6.7 collective-permute-done
  619.2 6.7 collective-permute-done
  627.8 6.7 collective-permute-done
  636.4 6.7 collective-permute-done
  645.0 6.7 collective-permute-done
  653.6 6.7 collective-permute-done
  662.2 20.9 %collective-permute-done = bf16[64,1024]{1,0:T(8,128)(2,1)S(1)} collective-permute-done((bf16[64,1024]{1,0:T(8,128)(2,1)}, bf16[64,1024]{1,0:T(8,128)(2,1)S(1)}, u32[]{:S(2)}, u32[]{:S(2)}) %collective-permute-start) | collective-permute-done | bytes 131104 | tf_op jit(solution)/shard_map/while/body/eval_jaxpr/ppermute | solution.py:12
  687.4 4.6 collective-permute-done
  693.0 15.3 %all_gather.7 = bf16[2,128,1024]{2,1,0:T(8,128)(2,1)S(1)} all-gather(bf16[2,64,1024]{2,1,0:T(8,128)(2,1)S(1)} %pad_maximum_fusion.1), channel_id=1, replica_groups=mesh['layer'=32,'dp'=8,'mp'=2] {'mp'}, dimensions={1}, use_global_device_ids=true | all-gather | bytes 786432 | tf_op jit(solution)/shard_map/all_gather | solution.py:111
  711.8 69.2 %all-reduce.16.cloned.1.call-done = f32[128,1024]{1,0:T(8,128)} async-done(((f32[128,1024]{1,0:T(8,128)}), f32[128,1024]{1,0:T(8,128)}) %all-reduce.16.cloned.1.call-update) | async-done | bytes 524304 | tf_op jit(solution)/shard_map/psum | solution.py:62
  784.7 58.0 %all-reduce.18.cloned.1.call-done = f32[128,1024]{1,0:T(8,128)} async-done(((f32[128,1024]{1,0:T(8,128)}), f32[128,1024]{1,0:T(8,128)}) %all-reduce.18.cloned.1.call-update) | async-done | bytes 524304 | tf_op jit(solution)/shard_map/psum | solution.py:62
  845.9 58.2 %all-reduce.20.cloned.1.call-done = f32[128,1024]{1,0:T(8,128)} async-done(((f32[128,1024]{1,0:T(8,128)}), f32[128,1024]{1,0:T(8,128)}) %all-reduce.20.cloned.1.call-update) | async-done | bytes 524304 | tf_op jit(solution)/shard_map/psum | solution.py:62
  905.2 4.2 convert_bitcast_fusion
  909.3 7.9 copy.11
  917.2 5.5 copy.13
  924.9 52.1 %reduce-scatter.4.cloned.1.call-done = bf16[128,2048]{1,0:T(8,128)(2,1)} async-done(((bf16[1024,2048]{1,0:T(8,128)(2,1)}), bf16[128,2048]{1,0:T(8,128)(2,1)}) %reduce-scatter.4.cloned.1.call-update) | async-done | bytes 524304
  (182 shorter events, 115.2 us)
Async XLA Ops:
  10.7 100.9 %all-to-all-start = ((bf16[8,4,128,512]{3,2,1,0:T(8,128)(2,1)}), bf16[8,4,128,512]{3,2,1,0:T(8,128)(2,1)}, u32[]{:S(2)}, u32[]{:S(2)}) async-start(bf16[8,4,128,512]{3,2,1,0:T(8,128)(2,1)} %stack.48), calls=%async_computation | async-start | bytes 8388608 | tf_op jit(solution)/shard_map/all_to_all | solution.py:45
  18.5 163.9 %all-reduce.8.cloned.1.call-start = ((), (), s32[]{:S(2)}) async-start(), calls=%async_computation.3 | async-start | bytes 1048576 | tf_op jit(solution)/shard_map/psum | solution.py:62
  18.5 8.4 collective-permute-start.1
  115.2 68.4 %copy-start.2 = (bf16[1,8,128,512]{3,2,0,1:T(8,128)(2,1)}, bf16[1,8,128,512]{3,2,0,1:T(8,128)(2,1)S(1)}, u32[]{:S(2)}) copy-start(bf16[1,8,128,512]{3,2,0,1:T(8,128)(2,1)S(1)} %get-tuple-element.232) | copy-start | bytes 3145732
  117.9 125.9 %all-reduce.10.cloned.1.call-start = ((), (), s32[]{:S(2)}) async-start(), calls=%async_computation.4 | async-start | bytes 1048576 | tf_op jit(solution)/shard_map/psum | solution.py:62
  119.2 66.5 %copy-start.16 = (f32[128,512]{1,0:T(8,128)}, f32[128,512]{1,0:T(8,128)S(1)}, u32[]{:S(2)}) copy-start(f32[128,512]{1,0:T(8,128)S(1)} %fusion.54) | copy-start | bytes 786436
  119.2 66.6 %copy-start.8 = (bf16[4,128,1024]{2,1,0:T(8,128)(2,1)S(1)}, bf16[4,128,1024]{2,1,0:T(8,128)(2,1)}, u32[]{:S(2)}) copy-start(bf16[4,128,1024]{2,1,0:T(8,128)(2,1)} %param.10) | copy-start | bytes 3145732
  185.8 119.3 %all-reduce.12.cloned.1.call-start = ((), (), s32[]{:S(2)}) async-start(), calls=%async_computation.5 | async-start | bytes 1048576 | tf_op jit(solution)/shard_map/psum | solution.py:62
  247.0 125.3 %all-gather.2.cloned.1.call-start = ((), (), s32[]{:S(2)}) async-start(), calls=%async_computation.2 | async-start | bytes 3145728 | tf_op jit(solution)/shard_map/all_gather | solution.py:75
  247.6 185.4 %all-reduce.14.cloned.1.call-start = ((), (), s32[]{:S(2)}) async-start(), calls=%async_computation.6 | async-start | bytes 1048576 | tf_op jit(solution)/shard_map/psum | solution.py:62
  306.4 65.9 %slice-start = ((bf16[4,128,1024]{2,1,0:T(8,128)(2,1)}), bf16[1,128,1024]{2,1,0:T(8,128)(2,1)S(1)}, s32[]{:S(2)}) async-start(bf16[4,128,1024]{2,1,0:T(8,128)(2,1)} %param.10), calls=%async_computation.11 | async-start | bytes 524288 | tf_op jit(solution)/shard_map/slice | solution.py:76
  308.8 472.2 %all-reduce.16.cloned.1.call-start = ((), (), s32[]{:S(2)}) async-start(), calls=%async_computation.7 | async-start | bytes 1048576 | tf_op jit(solution)/shard_map/psum | solution.py:62
  372.2 62.6 %copy-start = (bf16[1,1024,1024]{2,1,0:T(8,128)(2,1)S(1)}, bf16[1,1024,1024]{2,1,0:T(8,128)(2,1)}, u32[]{:S(2)}) copy-start(bf16[1,1024,1024]{2,1,0:T(8,128)(2,1)} %all-gather.2.cloned.1.call-done) | copy-start | bytes 6291460
  434.8 6.8 collective-permute-start
  441.7 6.5 collective-permute-start
  448.1 6.5 collective-permute-start
  454.6 6.5 collective-permute-start
  461.1 6.5 collective-permute-start
  467.6 6.5 collective-permute-start
  474.1 6.5 collective-permute-start
  480.6 6.5 collective-permute-start
  487.1 6.5 collective-permute-start
  493.6 6.5 collective-permute-start
  500.0 6.5 collective-permute-start
  506.5 7.6 collective-permute-start
  514.1 8.6 collective-permute-start
  522.7 8.6 collective-permute-start
  531.3 8.6 collective-permute-start
  539.9 8.6 collective-permute-start
  548.5 8.6 collective-permute-start
  557.1 8.6 collective-permute-start
  565.7 8.6 collective-permute-start
  574.3 8.6 collective-permute-start
  582.9 8.6 collective-permute-start
  591.5 8.6 collective-permute-start
  600.1 8.6 collective-permute-start
  608.7 8.6 collective-permute-start
  617.3 8.6 collective-permute-start
  625.9 8.6 collective-permute-start
  634.5 8.6 collective-permute-start
  643.1 8.6 collective-permute-start
  651.7 8.6 collective-permute-start
  660.3 22.8 %collective-permute-start = (bf16[64,1024]{1,0:T(8,128)(2,1)}, bf16[64,1024]{1,0:T(8,128)(2,1)S(1)}, u32[]{:S(2)}, u32[]{:S(2)}) collective-permute-start(bf16[64,1024]{1,0:T(8,128)(2,1)} %bitcast.134), channel_id=1, source_target_pairs={{16,0},{32,16},{48,32},{64,48},{80,64},{96,80},{112,96},{128,112},... | collective-permute-start | bytes 393224 | tf_op jit(solution)/shard_map/while/body/eval_jaxpr/ppermute | solution.py:12
  685.4 6.5 collective-permute-start
  710.5 72.9 %copy-start.3 = (bf16[1,8,128,512]{3,2,0,1:T(8,128)(2,1)S(1)}, bf16[1,8,128,512]{3,2,0,1:T(8,128)(2,1)}, u32[]{:S(2)}) copy-start(bf16[1,8,128,512]{3,2,0,1:T(8,128)(2,1)} %copy-done.2) | copy-start | bytes 3145732
  711.8 130.9 %all-reduce.18.cloned.1.call-start = ((), (), s32[]{:S(2)}) async-start(), calls=%async_computation.8 | async-start | bytes 1048576 | tf_op jit(solution)/shard_map/psum | solution.py:62
  784.7 119.4 %all-reduce.20.cloned.1.call-start = ((), (), s32[]{:S(2)}) async-start(), calls=%async_computation.9 | async-start | bytes 1048576 | tf_op jit(solution)/shard_map/psum | solution.py:62
  845.8 131.2 %reduce-scatter.4.cloned.1.call-start = ((), (), s32[]{:S(2)}) async-start(), calls=%async_computation.10 | async-start | bytes 4718592
  (24 other events, 449.2 us)
Sparse Core Ops, SparseCore 0:
  118.0 64.3 all-reduce.7
  185.9 57.8 all-reduce.9
  247.1 57.9 all-reduce.11
  307.6 64.5 all-gather.1
  375.0 57.9 all-reduce.13
  711.9 69.1 all-reduce.15
  784.8 57.8 all-reduce.17
  846.1 57.8 all-reduce.19
  922.9 54.0 reduce-scatter.3
